TPU v7x, 512 devices: a whole 4x4x16 slice. The times are simulated.
512 devices in a mesh: seq: 16 (over z), blk: 32 (over y, x, core).
Axes of the slice: x: 4, y: 4, z: 16, core: 2. Of those that a mesh axis runs over, the one named last changes fastest.
Arguments:
- train_acts: bfloat16 [65536, 4096], P(('seq', 'blk')), may hold values from -6 to 6
- train_grads: bfloat16 [65536, 14336], P(('seq', 'blk')), may hold values from -0.0234375 to 0.0234375
- block_table: int32 [32, 2], replicated, may hold values from 0 to 55, as said below
- seq_lengths: int32 [64], replicated, may hold values from 256 to 1024, as said below
- query_acts: bfloat16 [32, 256, 256], P('blk', 'seq'), may hold values from -6 to 6
- query_grads: bfloat16 [32, 256, 256], P('blk', 'seq'), may hold values from -6 to 6
- basis_acts: bfloat16 [32, 256, 256], P('blk', 'seq'), may hold values from -0.375 to 0.375
- basis_grads: bfloat16 [32, 256, 256], P('blk', 'seq'), may hold values from -0.375 to 0.375
- eigenvalues: float32 [32, 256, 256], P('blk', 'seq'), may hold values from 0.05 to 5
Outputs:
- scores: float32 [8, 65536], P(None, ('seq', 'blk'))
Inputs may be any that keep to these rules, and one draw needn't show every extreme that they name: `block_table`: column 0 of a row is an output-gradient block below 56, column 1 an activation block below 16; the last gradient block is named by some row. `seq_lengths`: some sequence has all 1024 tokens and some other one a quarter of them.
All inputs are finite; a program needn't handle non-finite values.
Results may differ from a plain program's by a relative error of at most 0.02.
Values may be sent and summed in bfloat16 or wider, within the bound.
A program may use at most 64 MiB of HBM per device.

v0:
```python
import math

import jax
import jax.numpy as jnp
from jax import lax
from jax.sharding import PartitionSpec as P

BLOCK = 256
SEQ_LEN = 1024
QUERIES = 8
QTOK = 32


DAMPING = 0.1


def score_rows(rot_acts, rot_grads, right_mat):
    total_rows = rot_acts.shape[0]
    block_rows = math.gcd(total_rows, 512)

    def block_scores(pieces):
        act_piece, grad_piece = pieces
        mixed = jnp.dot(act_piece, right_mat, preferred_element_type=jnp.float32).reshape(
            -1, QUERIES, BLOCK
        )
        return jnp.sum(mixed * grad_piece.astype(jnp.float32)[:, None, :], axis=2)

    blocks = lax.map(
        block_scores,
        (rot_acts.reshape(-1, block_rows, BLOCK), rot_grads.reshape(-1, block_rows, BLOCK)),
    )
    return blocks.reshape(total_rows, QUERIES)


def on_device(
    train_acts,
    train_grads,
    block_table,
    seq_lengths,
    query_acts,
    query_grads,
    basis_acts,
    basis_grads,
    eigenvalues,
):
    gathered = (
        lax.all_gather(basis_acts, "seq", axis=1, tiled=True),
        lax.all_gather(basis_grads, "seq", axis=1, tiled=True),
        lax.all_gather(query_acts, "seq", axis=1, tiled=True),
        lax.all_gather(query_grads, "seq", axis=1, tiled=True),
    )
    eigen_full = lax.all_gather(eigenvalues, "seq", axis=1, tiled=True)
    basis_act = gathered[0][0]
    basis_grad = gathered[1][0]
    qrot_acts = jnp.dot(gathered[2][0], basis_act, preferred_element_type=jnp.float32).astype(
        jnp.bfloat16
    )
    qrot_grads = jnp.dot(gathered[3][0], basis_grad, preferred_element_type=jnp.float32).astype(
        jnp.bfloat16
    )
    qrot_acts = qrot_acts.reshape(QUERIES, QTOK, BLOCK)
    qrot_grads = qrot_grads.reshape(QUERIES, QTOK, BLOCK)
    outer = jnp.einsum("qsi,qsj->jqi", qrot_grads, qrot_acts, preferred_element_type=jnp.float32)
    divisor = eigen_full[0].T[:, None, :] + DAMPING
    right_mat = (outer / QTOK / divisor).astype(jnp.bfloat16).reshape(BLOCK, QUERIES * BLOCK)
    tok_dev = train_acts.shape[0]
    act_blocks = train_acts.reshape(tok_dev, -1, BLOCK)
    grad_blocks = train_grads.reshape(tok_dev, -1, BLOCK)
    act_sel = jnp.take(act_blocks, block_table[:, 1], axis=1)
    grad_sel = jnp.take(grad_blocks, block_table[:, 0], axis=1)
    slices = jnp.concatenate([act_sel, grad_sel], axis=2)
    received = lax.all_to_all(slices, "blk", split_axis=1, concat_axis=1, tiled=True)
    joined = received.reshape(-1, 2 * BLOCK)
    rot_acts = jnp.dot(joined[:, :BLOCK], basis_act, preferred_element_type=jnp.float32).astype(
        jnp.bfloat16
    )
    rot_grads = jnp.dot(joined[:, BLOCK:], basis_grad, preferred_element_type=jnp.float32).astype(
        jnp.bfloat16
    )
    owner_terms = score_rows(rot_acts, rot_grads, right_mat).reshape(
        received.shape[0], received.shape[1], QUERIES
    )
    own_scores = lax.psum_scatter(
        owner_terms.astype(jnp.bfloat16), "blk", scatter_dimension=1, tiled=True
    ).astype(jnp.float32)[:, 0, :]
    base_index = (lax.axis_index("seq") * lax.axis_size("blk") + lax.axis_index("blk")) * tok_dev
    position = base_index + jnp.arange(tok_dev, dtype=jnp.int32)
    valid = position % SEQ_LEN < seq_lengths[position // SEQ_LEN]
    return jnp.where(valid[None, :], own_scores.T, jnp.zeros((), jnp.float32))


def solution(mesh):
    in_specs = (
        P(("seq", "blk"), None),
        P(("seq", "blk"), None),
        P(),
        P(),
        P("blk", "seq", None),
        P("blk", "seq", None),
        P("blk", "seq", None),
        P("blk", "seq", None),
        P("blk", "seq", None),
    )
    out_specs = P(None, ("seq", "blk"))
    return jax.shard_map(
        on_device, mesh=mesh, in_specs=in_specs, out_specs=out_specs, check_vma=False
    )
```

profile of v0, /device:TPU:1, one launch (start us, length us, event | category | flops | bytes accessed | tf_op | source)
XLA Modules:
  0.0 347.9 jit_solution(14030570702138324672)
XLA Ops:
  6.5 0.0 copy-start
  6.5 0.8 fusion.15
  7.3 0.8 and_bitcast_fusion.1
  8.1 6.1 %copy.22 = bf16[128,14336]{0,1:T(8,128)(2,1)} copy(bf16[128,14336]{1,0:T(8,128)(2,1)} %param.12) | data formatting | bytes 7340032 | tf_op args[1]
  14.1 6.0 %copy.23 = bf16[128,56,256]{2,0,1:T(8,128)(2,1)} copy(bf16[128,56,256]{0,2,1:T(8,128)(2,1)} %bitcast.79) | data formatting | bytes 7340032 | tf_op jit(solution)/shard_map/reshape | solution.py:68
  20.1 0.0 copy-done.2
  20.1 0.7 copy.20
  20.8 0.5 copy.21
  21.3 2.7 gather_fusion.2
  24.1 1.6 select_bitcast_fusion
  25.7 0.7 gather_fusion.1
  26.3 0.0 copy-start.1
  26.4 0.3 select_bitcast_fusion.1
  26.6 1.3 copy-done.1
  27.9 2.3 pad_maximum_fusion
  30.3 0.0 copy-start.3
  30.3 11.5 %all-to-all-start = ((bf16[128,32,512]{2,0,1:T(8,128)(2,1)}), bf16[128,32,512]{2,0,1:T(8,128)(2,1)}, u32[]{:S(2)}, u32[]{:S(2)}) async-start(bf16[128,32,512]{2,0,1:T(8,128)(2,1)} %pad_maximum_fusion), calls=%async_computation | async-start | bytes 8388608 | tf_op jit(solution)/shard_map/all_to_all | solution.py:72
  41.8 0.0 all-reduce.3.cloned.1.call-start
  41.9 0.0 copy-done
  41.9 1.2 gather_fusion
  43.1 29.4 %all_gather.15 = bf16[1,256,256]{2,1,0:T(8,128)(2,1)S(1)} all-gather(bf16[1,16,256]{2,1,0:T(8,128)(2,1)S(1)} %copy-done.4), channel_id=1, replica_groups=mesh['seq'=16,'blk'=32] {'seq'}, dimensions={1}, use_global_device_ids=true | all-gather | bytes 139264 | tf_op jit(solution)/shard_map/all_gather | solution.py:47
  72.5 22.5 %all_gather.18 = bf16[1,256,256]{2,1,0:T(8,128)(2,1)S(1)} all-gather(bf16[1,16,256]{2,1,0:T(8,128)(2,1)S(1)} %copy-done.5), channel_id=1, replica_groups=mesh['seq'=16,'blk'=32] {'seq'}, dimensions={1}, use_global_device_ids=true | all-gather | bytes 139264 | tf_op jit(solution)/shard_map/all_gather | solution.py:48
  95.0 21.4 %all_gather.16 = bf16[1,256,256]{2,1,0:T(8,128)(2,1)S(1)} all-gather(bf16[1,16,256]{2,1,0:T(8,128)(2,1)S(1)} %copy-done.6), channel_id=1, replica_groups=mesh['seq'=16,'blk'=32] {'seq'}, dimensions={1}, use_global_device_ids=true | all-gather | bytes 139264 | tf_op jit(solution)/shard_map/all_gather | solution.py:49
  116.4 0.0 copy-done.7
  116.4 20.4 %all_gather.17 = bf16[1,256,256]{2,1,0:T(8,128)(2,1)S(1)} all-gather(bf16[1,16,256]{2,1,0:T(8,128)(2,1)S(1)} %copy-done.7), channel_id=1, replica_groups=mesh['seq'=16,'blk'=32] {'seq'}, dimensions={1}, use_global_device_ids=true | all-gather | bytes 139264 | tf_op jit(solution)/shard_map/all_gather | solution.py:50
  136.8 21.0 %all_gather.19 = f32[1,256,256]{2,1,0:T(8,128)S(1)} all-gather(f32[1,16,256]{2,1,0:T(8,128)S(1)} %copy-done.3), channel_id=1, replica_groups=mesh['seq'=16,'blk'=32] {'seq'}, dimensions={1}, use_global_device_ids=true | all-gather | bytes 278528 | tf_op jit(solution)/shard_map/all_gather | solution.py:52
  157.8 0.2 convolution_convert_fusion.3
  158.0 0.2 convolution_convert_fusion.2
  158.3 1.5 divide_convert_fusion
  159.8 0.0 all-to-all-done
  159.8 4.5 %copy.24 = bf16[128,32,512]{2,1,0:T(8,128)(2,1)S(1)} copy(bf16[128,32,512]{2,0,1:T(8,128)(2,1)} %all-to-all-done) | data formatting | bytes 8388608 | tf_op jit(solution)/shard_map/all_to_all | solution.py:72
  164.3 2.0 convolution_convert_fusion.1
  166.4 0.7 convolution_convert_fusion
  167.1 18.8 %while.10 = (s32[]{:T(128)}, bf16[8,512,8]{1,2,0:T(8,128)(2,1)S(1)}, bf16[8,512,256]{2,1,0:T(8,128)(2,1)}, bf16[256,2048]{0,1:T(8,128)(2,1)}, bf16[8,512,256]{2,1,0:T(8,128)(2,1)S(1)}, /*index=5*/s32[]{:T(128)}) while((s32[]{:T(128)}, bf16[8,512,8]{1,2,0:T(8,128)(2,1)S(1)}, bf16[8,512,256]{2,1,0:T(8,128)(2,1)}, bf16[256,2048]{0,1:T(8,128)(2,1)}, ...), condition=%wide.region_2.3_spmd, body=%wide.region_0.0_spmd.sunk | while | flops 539095040 | bytes 3695181 | solution.py:28
  167.1 0.1 copy.30
  167.3 0.1 bitcast_convert_fusion.2
  167.3 2.1 multiply_reduce_fusion.2
  169.5 0.1 copy.30
  169.6 0.1 bitcast_convert_fusion.2
  169.7 2.1 multiply_reduce_fusion.2
  171.8 0.1 copy.30
  172.0 0.1 bitcast_convert_fusion.2
  172.0 2.1 multiply_reduce_fusion.2
  174.2 0.1 copy.30
  174.3 0.1 bitcast_convert_fusion.2
  174.4 2.1 multiply_reduce_fusion.2
  176.5 0.1 copy.30
  176.7 0.1 bitcast_convert_fusion.2
  176.7 2.1 multiply_reduce_fusion.2
  178.9 0.1 copy.30
  179.0 0.1 bitcast_convert_fusion.2
  179.1 2.1 multiply_reduce_fusion.2
  181.2 0.1 copy.30
  181.4 0.1 bitcast_convert_fusion.2
  181.4 2.1 multiply_reduce_fusion.2
  183.5 0.1 copy.30
  183.7 0.1 bitcast_convert_fusion.2
  183.8 2.1 multiply_reduce_fusion.2
  185.9 0.2 convert_element_type.42
  186.1 0.8 copy.27
  186.8 0.0 all-reduce.3.cloned.1.call-update
  186.9 1.3 dynamic-slice
  188.2 150.9 %all-reduce.3.cloned.1.call-done = bf16[128,32,8]{0,2,1:T(8,128)(2,1)} async-done(((bf16[128,32,8]{0,2,1:T(8,128)(2,1)}), bf16[128,32,8]{0,2,1:T(8,128)(2,1)}) %all-reduce.3.cloned.1.call-update) | async-done | bytes 65552
  339.1 2.0 fusion.11
  (32 shorter events, 0.4 us)
Async XLA Ops:
  6.5 35.3 %copy-start = (s32[64]{0:T(128)S(1)}, s32[64]{0:T(128)}, u32[]{:S(2)}) copy-start(s32[64]{0:T(128)} %param.14) | copy-start | bytes 772
  14.1 6.0 %copy-start.2 = (bf16[128,4096]{1,0:T(8,128)(2,1)S(1)}, bf16[128,4096]{1,0:T(8,128)(2,1)}, u32[]{:S(2)}) copy-start(bf16[128,4096]{1,0:T(8,128)(2,1)} %param.11) | copy-start | bytes 3145732
  26.3 1.6 copy-start.1
  30.3 12.8 %copy-start.4 = (bf16[1,16,256]{2,1,0:T(8,128)(2,1)S(1)}, bf16[1,16,256]{2,1,0:T(8,128)(2,1)}, u32[]{:S(2)}) copy-start(bf16[1,16,256]{2,1,0:T(8,128)(2,1)} %param.17) | copy-start | bytes 24580
  30.3 42.2 %copy-start.5 = (bf16[1,16,256]{2,1,0:T(8,128)(2,1)S(1)}, bf16[1,16,256]{2,1,0:T(8,128)(2,1)}, u32[]{:S(2)}) copy-start(bf16[1,16,256]{2,1,0:T(8,128)(2,1)} %param.18) | copy-start | bytes 24580
  30.3 64.7 %copy-start.6 = (bf16[1,16,256]{2,1,0:T(8,128)(2,1)S(1)}, bf16[1,16,256]{2,1,0:T(8,128)(2,1)}, u32[]{:S(2)}) copy-start(bf16[1,16,256]{2,1,0:T(8,128)(2,1)} %param.15) | copy-start | bytes 24580
  30.3 86.1 %copy-start.7 = (bf16[1,16,256]{2,1,0:T(8,128)(2,1)S(1)}, bf16[1,16,256]{2,1,0:T(8,128)(2,1)}, u32[]{:S(2)}) copy-start(bf16[1,16,256]{2,1,0:T(8,128)(2,1)} %param.16) | copy-start | bytes 24580
  30.3 106.5 %copy-start.3 = (f32[1,16,256]{2,1,0:T(8,128)S(1)}, f32[1,16,256]{2,1,0:T(8,128)}, u32[]{:S(2)}) copy-start(f32[1,16,256]{2,1,0:T(8,128)} %param.19) | copy-start | bytes 49156
  30.3 129.5 %all-to-all-start = ((bf16[128,32,512]{2,0,1:T(8,128)(2,1)}), bf16[128,32,512]{2,0,1:T(8,128)(2,1)}, u32[]{:S(2)}, u32[]{:S(2)}) async-start(bf16[128,32,512]{2,0,1:T(8,128)(2,1)} %pad_maximum_fusion), calls=%async_computation | async-start | bytes 8388608 | tf_op jit(solution)/shard_map/all_to_all | solution.py:72
  41.8 297.3 %all-reduce.3.cloned.1.call-start = ((), (), s32[]{:S(2)}) async-start(), calls=%async_computation.1 | async-start | bytes 131072
Sparse Core Ops, SparseCore 0:
  187.0 152.0 all-reduce.2
where the time goes:
time: 349 us; the launch traced here: 348 us
  waiting for transfers between devices  151 us (43%)
  blocking collectives  115 us (33%)
  local copies, waits for them, and re-layouts  27.4 us (8%)
  matrix products  21.2 us (6%)
  between operations  13.6 us (4%)
  starting transfers between devices  11.5 us (3%)
  other arithmetic  8.15 us (2%)
    unnamed x2, waiting for transfers between devices  151 us
    all_gather x1, blocking collectives, on_device(): lax.all_gather(basis_acts, 'seq', axis=1, tiled=True)  29.4 us
    all_gather x1, blocking collectives, on_device(): lax.all_gather(basis_grads, 'seq', axis=1, tiled=True)  22.5 us
    all_gather x1, blocking collectives, on_device(): lax.all_gather(query_acts, 'seq', axis=1, tiled=True)  21.4 us
    all_gather x1, blocking collectives, on_device(): eigen_full = lax.all_gather(eigenvalues, 'seq', axis=1, tiled=True)  21 us
    all_gather x1, blocking collectives, on_device(): lax.all_gather(query_grads, 'seq', axis=1, tiled=True)  20.4 us
    dot_general x8, matrix products, block_scores(): jnp.dot(act_piece, right_mat, preferred_element_type=jnp.float32)  16.6 us
    all_to_all x1, starting transfers between devices, on_device(): lax.all_to_all(slices, 'blk', split_axis=1, concat_axis=1, tiled=True)  11.5 us
  transfers between devices with their start and end apart: 2, of which 1 were waited for; matrix products, arithmetic and copies ran while one was open for 1% of the time, Pallas kernels for 0%

commit v1 on v0

v1 whole, which is shorter than its diff:
```python
import jax
import jax.numpy as jnp
from jax import lax
from jax.experimental import pallas as pl
from jax.experimental.pallas import tpu as pltpu
from jax.sharding import PartitionSpec as P

BLOCK = 256
SEQ_LEN = 1024
QUERIES = 8
QTOK = 32
DAMPING = 0.1
MESH = pl.DeviceIdType.MESH

NX, NY, NC = 4, 4, 2
CHIPS = NX * NY
NB = CHIPS * NC
NZ = 16
SHARD = 16
TOK = 128

HOPS = (0, 1, 2, 1)
FAR_FIRST = sorted(
    [(dy, dx) for dy in range(NY) for dx in range(NX)],
    key=lambda o: -(HOPS[o[0]] + HOPS[o[1]]),
)
WORK_ORDER = [(0, 0)] + FAR_FIRST[:-1]


def pick(step, values):
    result = 0
    for place, value in enumerate(values):
        result = result + jnp.where(step == place, value, 0)
    return result


def kernel(
    acts_hbm, grads_hbm, table, qa_ref, qg_ref, ba_ref, bg_ref, eig_ref,
    out_ref,
    acts, grads, send, recv, weights, act_t, grad_t, right, ret_send, ret_recv,
    load_sem, send_sem, recv_sem, up_sem, down_sem, ring_sem, back_sem, home_sem,
):
    z = lax.axis_index("seq")
    b = lax.axis_index("blk")
    chip = b // NC
    core = b % NC
    y, x = chip // NX, chip % NX
    above, below = (z + 1) % NZ, (z + NZ - 1) % NZ

    for hbm, blocks, sem in ((acts_hbm, acts, 0), (grads_hbm, grads, 1)):

        @pl.loop(0, blocks.shape[0])
        def _(block):
            columns = pl.ds(pl.multiple_of(block * BLOCK, BLOCK), BLOCK)
            pltpu.make_async_copy(hbm.at[:, columns], blocks.at[block], load_sem.at[sem]).start()

    barrier = pltpu.get_barrier_semaphore()

    @pl.loop(1, NB)
    def _(step):
        pl.semaphore_signal(barrier, inc=1, device_id=(z, (b + step) % NB), device_id_type=MESH)

    pl.semaphore_signal(barrier, inc=1, device_id=(above, b), device_id_type=MESH)
    pl.semaphore_signal(barrier, inc=1, device_id=(below, b), device_id_type=MESH)

    weights[z, 0:16] = ba_ref[0]
    weights[z, 16:32] = bg_ref[0]
    weights[z, 32:48] = qa_ref[0]
    weights[z, 48:64] = qg_ref[0]
    weights[z, 64:80] = (eig_ref[0] + DAMPING).astype(jnp.bfloat16)

    pl.semaphore_wait(barrier, NB + 1)

    def ring_up(step):
        slot = (z + NZ - step) % NZ
        return pltpu.make_async_remote_copy(
            weights.at[slot], weights.at[slot], up_sem.at[step], ring_sem.at[slot],
            device_id=(above, b), device_id_type=MESH)

    def ring_down(step):
        slot = (z + step) % NZ
        return pltpu.make_async_remote_copy(
            weights.at[slot], weights.at[slot], down_sem.at[step], ring_sem.at[slot],
            device_id=(below, b), device_id_type=MESH)

    ring_up(0).start()
    ring_down(0).start()
    for blocks, sem in ((acts, 0), (grads, 1)):
        pltpu.make_async_copy(blocks, blocks, load_sem.at[sem]).wait()

    def token_copy(peer):
        return pltpu.make_async_remote_copy(
            send.at[peer], recv.at[b], send_sem.at[peer], recv_sem.at[b],
            device_id=(z, peer), device_id_type=MESH)

    def select(owner):
        return acts[table[owner, 1]], grads[table[owner, 0]]

    @pl.loop(0, CHIPS)
    def _(step):
        offset = pick(step, [dy * NX + dx for dy, dx in FAR_FIRST])
        to_chip = ((y + offset // NX) % NY) * NX + (x + offset % NX) % NX
        for c in range(NC):
            peer = to_chip * NC + c
            act_sel, grad_sel = select(peer)

            @pl.when(peer != b)
            def _():
                send[peer, :, 0:BLOCK] = act_sel
                send[peer, :, BLOCK : 2 * BLOCK] = grad_sel
                token_copy(peer).start()

            @pl.when(peer == b)
            def _():
                recv[peer, :, 0:BLOCK] = act_sel
                recv[peer, :, BLOCK : 2 * BLOCK] = grad_sel

    def arrived(slot):
        pltpu.make_async_remote_copy(
            weights.at[slot], weights.at[slot], up_sem.at[0], ring_sem.at[slot],
            device_id=(above, b), device_id_type=MESH).wait_recv()

    @pl.loop(1, NZ // 2)
    def _(step):
        arrived((z + NZ - step) % NZ)
        ring_up(step).start()
        arrived((z + step) % NZ)

        @pl.when(step < NZ // 2 - 1)
        def _():
            ring_down(step).start()

    arrived((z + NZ // 2) % NZ)

    def gathered(place):
        return weights[:, place * SHARD : (place + 1) * SHARD, :].reshape(BLOCK, BLOCK)

    def dot(lhs, rhs, dims):
        return lax.dot_general(lhs, rhs, (dims, ((), ())), preferred_element_type=jnp.float32)

    basis_act, basis_grad = gathered(0), gathered(1)
    act_t[...] = basis_act.astype(jnp.float32).T.astype(jnp.bfloat16)
    grad_t[...] = basis_grad.astype(jnp.float32).T.astype(jnp.bfloat16)
    qrot_acts = dot(gathered(2), basis_act, ((1,), (0,))).astype(jnp.bfloat16)
    qrot_grads = dot(gathered(3), basis_grad, ((1,), (0,))).astype(jnp.bfloat16)
    scale = 1.0 / (gathered(4).astype(jnp.float32) * QTOK)
    for q in range(QUERIES):
        rows = slice(q * QTOK, (q + 1) * QTOK)
        outer = dot(qrot_grads[rows], qrot_acts[rows], ((0,), (0,)))
        right[q * BLOCK : (q + 1) * BLOCK, :] = (outer * scale).astype(jnp.bfloat16)

    def return_copy(peer):
        return pltpu.make_async_remote_copy(
            ret_send.at[peer], ret_recv.at[b], back_sem.at[peer], home_sem.at[b],
            device_id=(z, peer), device_id_type=MESH)

    @pl.loop(0, CHIPS)
    def _(step):
        offset = pick(step, [dy * NX + dx for dy, dx in WORK_ORDER])
        from_chip = ((y + NY - offset // NX) % NY) * NX + (x + NX - offset % NX) % NX
        for c in range(NC):
            peer = from_chip * NC + c

            @pl.when(peer != b)
            def _():
                pltpu.make_async_remote_copy(
                    send.at[peer], recv.at[peer], send_sem.at[peer], recv_sem.at[peer],
                    device_id=(z, peer), device_id_type=MESH).wait_recv()

        tokens = recv[pl.ds(from_chip * NC, NC)].reshape(NC * TOK, 2 * BLOCK)
        rot_acts = dot(act_t[...], tokens[:, 0:BLOCK], ((1,), (1,))).astype(jnp.bfloat16)
        rot_grads = dot(grad_t[...], tokens[:, BLOCK:], ((1,), (1,))).astype(jnp.bfloat16)
        rot_grads = rot_grads.astype(jnp.float32)
        for q in range(QUERIES):
            mixed = dot(right[q * BLOCK : (q + 1) * BLOCK, :], rot_acts, ((1,), (0,)))
            score = jnp.sum(mixed * rot_grads, axis=0, keepdims=True)
            for c in range(NC):
                ret_send[from_chip * NC + c, q : q + 1, :] = score[:, c * TOK : (c + 1) * TOK]
        for c in range(NC):
            peer = from_chip * NC + c

            @pl.when(peer != b)
            def _():
                return_copy(peer).start()

    ret_recv[b] = ret_send[b]

    @pl.loop(1, NB)
    def _(step):
        peer = (b + step) % NB
        pltpu.make_async_remote_copy(
            ret_send.at[peer], ret_recv.at[peer], back_sem.at[peer], home_sem.at[peer],
            device_id=(z, peer), device_id_type=MESH).wait_recv()

    total = ret_recv[0]
    for source in range(1, NB):
        total = total + ret_recv[source]
    out_ref[...] = total

    @pl.loop(1, NB)
    def _(step):
        peer = (b + step) % NB
        token_copy(peer).wait_send()
        return_copy(peer).wait_send()

    @pl.loop(0, NZ // 2)
    def _(step):
        ring_up(step).wait_send()

    @pl.loop(0, NZ // 2 - 1)
    def _(step):
        ring_down(step).wait_send()


def on_device(
    train_acts, train_grads, block_table, seq_lengths,
    query_acts, query_grads, basis_acts, basis_grads, eigenvalues,
):
    bf16, f32 = jnp.bfloat16, jnp.float32
    vmem = pl.BlockSpec(memory_space=pltpu.VMEM)
    smem = pl.BlockSpec(memory_space=pltpu.SMEM)
    hbm = pl.BlockSpec(memory_space=pl.ANY)
    dma = pltpu.SemaphoreType.DMA
    scores = pl.pallas_call(
        kernel,
        out_shape=jax.ShapeDtypeStruct((QUERIES, TOK), f32),
        in_specs=[hbm, hbm, smem] + [vmem] * 5,
        out_specs=vmem,
        scratch_shapes=[
            pltpu.VMEM((train_acts.shape[1] // BLOCK, TOK, BLOCK), bf16),
            pltpu.VMEM((train_grads.shape[1] // BLOCK, TOK, BLOCK), bf16),
            pltpu.VMEM((NB, TOK, 2 * BLOCK), bf16),
            pltpu.VMEM((NB, TOK, 2 * BLOCK), bf16),
            pltpu.VMEM((NZ, 5 * SHARD, BLOCK), bf16),
            pltpu.VMEM((BLOCK, BLOCK), bf16),
            pltpu.VMEM((BLOCK, BLOCK), bf16),
            pltpu.VMEM((QUERIES * BLOCK, BLOCK), bf16),
            pltpu.VMEM((NB, QUERIES, TOK), f32),
            pltpu.VMEM((NB, QUERIES, TOK), f32),
            dma((2,)), dma((NB,)), dma((NB,)), dma((NZ // 2,)), dma((NZ // 2,)),
            dma((NZ,)), dma((NB,)), dma((NB,)),
        ],
        compiler_params=pltpu.CompilerParams(
            collective_id=0, has_side_effects=True, vmem_limit_bytes=48 * 2**20),
    )(train_acts, train_grads, block_table,
      query_acts, query_grads, basis_acts, basis_grads, eigenvalues)
    base = (lax.axis_index("seq") * NB + lax.axis_index("blk")) * TOK
    place = base % SEQ_LEN + lax.broadcasted_iota(jnp.int32, (QUERIES, TOK), 1)
    return jnp.where(place < seq_lengths[base // SEQ_LEN], scores, 0.0)


def solution(mesh):
    in_specs = (
        P(("seq", "blk"), None),
        P(("seq", "blk"), None),
        P(),
        P(),
        P("blk", "seq", None),
        P("blk", "seq", None),
        P("blk", "seq", None),
        P("blk", "seq", None),
        P("blk", "seq", None),
    )
    return jax.shard_map(
        on_device, mesh=mesh, in_specs=in_specs, out_specs=P(None, ("seq", "blk")),
        check_vma=False)
```

time: 349 us -> 89.2 us (0.26)
  waiting for transfers between devices: 151 us -> 0 us
  blocking collectives: 115 us -> 0 us
  Pallas kernels: 0 us -> 79 us
  matrix products: 21.2 us -> 0 us
  local copies, waits for them, and re-layouts: 27.4 us -> 8.13 us
  between operations: 13.6 us -> 0.05 us
  starting transfers between devices: 11.5 us -> 0 us
  other arithmetic: 8.15 us -> 1.25 us
    unnamed x2 -> x0, waiting for transfers between devices: 151 us -> none
    all_gather x5 -> x0, blocking collectives: 115 us -> none  [the longest x1 29.4 us: on_device(): lax.all_gather(basis_acts, 'seq', axis=1, tiled=True)]
    pallas_call x0 -> x1, Pallas kernels: none -> 79 us  [on_device(): pl.pallas_call(kernel, out_shape=jax.ShapeDtypeStruct((QUERIES, TOK), f32...]
    dot_general x13 -> x0, matrix products: 21.2 us -> none  [the longest x8 16.6 us: block_scores(): jnp.dot(act_piece, right_mat, preferred_element_type=jnp.float32)]
    all_to_all x1 -> x0, starting transfers between devices: 11.5 us -> none  [on_device(): lax.all_to_all(slices, 'blk', split_axis=1, concat_axis=1, tiled=True)]
    reshape x2 -> x0, local copies, waits for them, and re-layouts: 6.53 us -> none  [the longest x1 6 us: on_device(): grad_blocks = train_grads.reshape(tok_dev, -1, BLOCK)]
    gather x3 -> x0, local copies, waits for them, and re-layouts: 4.63 us -> none  [the longest x1 2.72 us: on_device(): grad_sel = jnp.take(grad_blocks, block_table[:, 0], axis=1)]
    all_to_all x1 -> x0, local copies, waits for them, and re-layouts: 4.53 us -> none  [on_device(): lax.all_to_all(slices, 'blk', split_axis=1, concat_axis=1, tiled=True)]
  transfers between devices with their start and end apart: 2 -> 0, of which waited for: 1 -> 0; matrix products, arithmetic and copies ran while one was open for 1% -> 0% of each run, Pallas kernels for 0% -> 0%
where the time goes in v1:
time: 89.2 us; the launch traced here: 88.4 us
  Pallas kernels  79 us (89%)
  local copies, waits for them, and re-layouts  8.13 us (9%)
  other arithmetic  1.25 us (1%)
    pallas_call x1, Pallas kernels, on_device(): pl.pallas_call(kernel, out_shape=jax.ShapeDtypeStruct((QUERIES, TOK), f32...  79 us
    unnamed x17, local copies, waits for them, and re-layouts  7.54 us

profile of v1, /device:TPU:1, one launch (start us, length us, event | category | flops | bytes accessed | tf_op | source)
XLA Modules:
  0.0 88.4 jit_solution(3387810553194396745)
XLA Ops:
  0.0 0.0 copy-start.7
  0.0 0.8 copy.10.table
  0.8 0.0 copy-start
  0.8 2.0 %copy-done = bf16[128,14336]{1,0:T(8,128)(2,1)S(1)} copy-done((bf16[128,14336]{1,0:T(8,128)(2,1)S(1)}, bf16[128,14336]{1,0:T(8,128)(2,1)}, u32[]{:S(2)}) %copy-start) | copy-done | bytes 3670040
  2.8 0.0 copy-start.1
  2.8 1.2 %copy-done.1 = bf16[128,4096]{1,0:T(8,128)(2,1)S(1)} copy-done((bf16[128,4096]{1,0:T(8,128)(2,1)S(1)}, bf16[128,4096]{1,0:T(8,128)(2,1)}, u32[]{:S(2)}) %copy-start.1) | copy-done | bytes 1048600
  4.0 0.0 copy-start.2
  4.0 0.7 copy-done.2
  4.8 0.0 copy-start.3
  4.8 0.7 copy-done.3
  5.5 0.0 copy-start.4
  5.5 0.7 copy-done.4
  6.2 0.0 copy-start.5
  6.2 0.7 copy-done.5
  6.8 0.0 copy-start.6
  6.9 0.7 copy-done.6
  7.5 79.0 %shard_map.91 = f32[8,128]{1,0:T(8,128)S(1)} custom-call(bf16[128,4096]{1,0:T(8,128)(2,1)S(1)} %copy-done.1, bf16[128,14336]{1,0:T(8,128)(2,1)S(1)} %copy-done, s32[32,2]{1,0:T(8,128)S(1)} %copy.10.table, bf16[1,16,256]{2,1,0:T(8,128)(2,1)S(1)} %copy-done.3, bf16[1,16,256]{2,1,0:T(8,128)(2,1)S(1)} %copy-done.4, bf16[1,16,256]{2,1,0:T(8,128)(2,1)S(1)} %copy-done.5, ...), custom_call_target="tpu_custom_call" | custom-call | tf_op jit(solution)/shard_map/pallas_call | solution.py:224
  86.5 0.0 copy-done.7
  86.5 0.6 dynamic_slice.3
  87.1 0.7 add_compare_fusion
  87.8 0.6 broadcast_select_fusion
Async XLA Ops:
  0.0 86.5 %copy-start.7 = (s32[64]{0:T(128)S(1)}, s32[64]{0:T(128)}, u32[]{:S(2)}) copy-start(s32[64]{0:T(128)} %param.12) | copy-start | bytes 772
  0.8 2.0 %copy-start = (bf16[128,14336]{1,0:T(8,128)(2,1)S(1)}, bf16[128,14336]{1,0:T(8,128)(2,1)}, u32[]{:S(2)}) copy-start(bf16[128,14336]{1,0:T(8,128)(2,1)} %grads_hbm.1) | copy-start | bytes 11010052
  2.8 1.2 %copy-start.1 = (bf16[128,4096]{1,0:T(8,128)(2,1)S(1)}, bf16[128,4096]{1,0:T(8,128)(2,1)}, u32[]{:S(2)}) copy-start(bf16[128,4096]{1,0:T(8,128)(2,1)} %acts_hbm.1) | copy-start | bytes 3145732
  4.0 0.7 copy-start.2
  4.8 0.7 copy-start.3
  5.5 0.7 copy-start.4
  6.2 0.7 copy-start.5
  6.8 0.7 copy-start.6

commit v2 on v0

v2 whole, which is shorter than its diff:
```python
import jax
import jax.numpy as jnp
from jax import lax
from jax.experimental import pallas as pl
from jax.experimental.pallas import tpu as pltpu
from jax.sharding import PartitionSpec as P

BLOCK = 256
SEQ_LEN = 1024
QUERIES = 8
QTOK = 32
DAMPING = 0.1
MESH = pl.DeviceIdType.MESH

SIDE = 4
NC = 2
NB = SIDE * SIDE * NC
NZ = 16
SHARD = 16
TOK = 128


def wrap(i, n=SIDE):
    return lax.rem(i + n, n)


def blk_of(y, x, core):
    return (wrap(y) * SIDE + wrap(x)) * NC + core


def dot(lhs, rhs, dims):
    return lax.dot_general(lhs, rhs, (dims, ((), ())), preferred_element_type=jnp.float32)


def kernel(
    acts_hbm, grads_hbm, qa_hbm, qg_hbm, ba_hbm, bg_hbm, eig_hbm, table, lengths,
    out_ref,
    acts, grads, eig, send, recv, weights, act_t, grad_t, right, scores, home,
    load_sem, shard_sem, send_sem, recv_sem, up_sem, down_sem, ring_sem,
    spread_sem, held_sem, back_sem, home_sem,
):
    z = lax.axis_index("seq")
    b = lax.axis_index("blk")
    core = lax.rem(b, NC)
    chip = lax.div(b, NC)
    y, x = lax.div(chip, SIDE), lax.rem(chip, SIDE)
    above, below = wrap(z + 1, NZ), wrap(z - 1, NZ)

    def holder(kind, j):
        return (z, blk_of(y + j, x, 0) if kind == 0 else blk_of(y, x + j, 1))

    def pair(kind, j, h):
        return blk_of(y + j, x + h, 0) if kind == 0 else blk_of(y + h, x + j, 1)

    def source(j, c):
        return (z, jnp.where(core == 0, blk_of(y - j, x, c), blk_of(y, x - j, c)))

    def fellow(h):
        return (z, jnp.where(core == 0, blk_of(y, x - h, 0), blk_of(y - h, x, 1)))

    shards = [
        pltpu.make_async_copy(
            hbm.at[0], weights.at[0, z, pl.ds(place * SHARD, SHARD)], shard_sem.at[place])
        for place, hbm in enumerate((ba_hbm, bg_hbm, qa_hbm, qg_hbm))
    ] + [pltpu.make_async_copy(eig_hbm.at[0], eig, shard_sem.at[4])]
    for copy in shards:
        copy.start()
    for hbm, blocks, sem in ((acts_hbm, acts, 0), (grads_hbm, grads, 1)):

        @pl.loop(0, blocks.shape[0])
        def _(block):
            columns = pl.ds(pl.multiple_of(block * BLOCK, BLOCK), BLOCK)
            pltpu.make_async_copy(hbm.at[:, columns], blocks.at[block], load_sem.at[sem]).start()

    barrier = pltpu.get_barrier_semaphore()
    greeted = [(z, blk_of(y, x, 1 - core)), (above, b), (below, b)]
    for j in range(1, SIDE):
        for c in range(NC):
            greeted += [(z, blk_of(y + j, x, c)), (z, blk_of(y, x + j, c))]
    for peer in greeted:
        pl.semaphore_signal(barrier, inc=1, device_id=peer, device_id_type=MESH)

    for copy in shards:
        copy.wait()
    weights[0, z, 4 * SHARD : 5 * SHARD] = (eig[...] + DAMPING).astype(jnp.bfloat16)
    pl.semaphore_wait(barrier, len(greeted))

    def ring(step, direction):
        slot, to, sems = (
            (wrap(z - step, NZ), above, up_sem) if direction > 0
            else (wrap(z + step, NZ), below, down_sem))
        piece = weights.at[0, slot]
        return pltpu.make_async_remote_copy(
            piece, piece, sems.at[step], ring_sem.at[slot],
            device_id=(to, b), device_id_type=MESH)

    def arrived(slot):
        piece = weights.at[0, slot]
        pltpu.make_async_remote_copy(
            piece, piece, up_sem.at[0], ring_sem.at[slot],
            device_id=(above, b), device_id_type=MESH).wait_recv()

    def spread(slot):
        for h in range(1, SIDE):
            pltpu.make_async_remote_copy(
                weights.at[0, slot], weights.at[h, slot], spread_sem.at[h], held_sem.at[h],
                device_id=fellow(h), device_id_type=MESH).start()

    def token_copy(kind, j, h):
        return pltpu.make_async_remote_copy(
            send.at[h, kind, j], recv.at[h, j, core], send_sem.at[h, kind, j],
            recv_sem.at[h, j, core], device_id=holder(kind, j), device_id_type=MESH)

    def dispatch(h):
        for j in (0, 2, 1, 3):
            for kind in range(NC):
                owner = pair(kind, j, h)
                act_sel, grad_sel = acts[table[1, owner]], grads[table[0, owner]]

                def to_peer():
                    send[h, kind, j, :, 0:BLOCK] = act_sel
                    send[h, kind, j, :, BLOCK : 2 * BLOCK] = grad_sel
                    token_copy(kind, j, h).start()

                def to_self():
                    recv[h, 0, core, :, 0:BLOCK] = act_sel
                    recv[h, 0, core, :, BLOCK : 2 * BLOCK] = grad_sel

                if j == 0:
                    pl.when(core != kind)(to_peer)
                    pl.when(core == kind)(to_self)
                else:
                    to_peer()

    ring(0, 1).start()
    ring(0, -1).start()
    spread(z)
    for blocks, sem in ((acts, 0), (grads, 1)):
        pltpu.make_async_copy(blocks, blocks, load_sem.at[sem]).wait()

    @pl.loop(1, NZ // 2)
    def _(step):
        @pl.when(step <= SIDE)
        def _():
            dispatch(step - 1)

        arrived(wrap(z - step, NZ))
        ring(step, 1).start()
        arrived(wrap(z + step, NZ))

        @pl.when(step < NZ // 2 - 1)
        def _():
            ring(step, -1).start()

        spread(wrap(z - step, NZ))
        spread(wrap(z + step, NZ))

    arrived(wrap(z + NZ // 2, NZ))
    spread(wrap(z + NZ // 2, NZ))

    def prepare(h):
        def gathered(place):
            rows = weights[h, :, place * SHARD : (place + 1) * SHARD, :]
            return rows.reshape(BLOCK, BLOCK)

        basis_act, basis_grad = gathered(0), gathered(1)
        act_t[...] = basis_act.astype(jnp.float32).T.astype(jnp.bfloat16)
        grad_t[...] = basis_grad.astype(jnp.float32).T.astype(jnp.bfloat16)
        qrot_acts = dot(gathered(2), basis_act, ((1,), (0,))).astype(jnp.bfloat16)
        qrot_grads = dot(gathered(3), basis_grad, ((1,), (0,))).astype(jnp.bfloat16)
        scale = 1.0 / (gathered(4).astype(jnp.float32) * QTOK)
        for q in range(QUERIES):
            rows = slice(q * QTOK, (q + 1) * QTOK)
            outer = dot(qrot_grads[rows], qrot_acts[rows], ((0,), (0,)))
            right[q * BLOCK : (q + 1) * BLOCK, :] = (outer * scale).astype(jnp.bfloat16)

    def return_copy(j, c):
        return pltpu.make_async_remote_copy(
            scores.at[j, c], home.at[core, j], back_sem.at[j, c], home_sem.at[core, j],
            device_id=source(j, c), device_id_type=MESH)

    def is_self(j, c):
        return jnp.logical_and(j == 0, c == core)

    @pl.loop(0, SIDE)
    def _(h):
        @pl.when(h > 0)
        def _():
            pltpu.make_async_remote_copy(
                weights.at[0], weights.at[h], spread_sem.at[h], held_sem.at[h],
                device_id=fellow(h), device_id_type=MESH).wait_recv()

        prepare(h)

        @pl.loop(0, SIDE)
        def _(j):
            for c in range(NC):

                @pl.when(jnp.logical_not(is_self(j, c)))
                def _():
                    pltpu.make_async_remote_copy(
                        send.at[h, 0, j], recv.at[h, j, c], send_sem.at[h, 0, j],
                        recv_sem.at[h, j, c], device_id=source(j, c),
                        device_id_type=MESH).wait_recv()

            tokens = recv[h, j].reshape(NC * TOK, 2 * BLOCK)
            rot_acts = dot(act_t[...], tokens[:, 0:BLOCK], ((1,), (1,))).astype(jnp.bfloat16)
            rot_grads = dot(grad_t[...], tokens[:, BLOCK:], ((1,), (1,))).astype(jnp.bfloat16)
            rot_grads = rot_grads.astype(jnp.float32)
            parts = []
            for q in range(QUERIES):
                mixed = dot(right[q * BLOCK : (q + 1) * BLOCK, :], rot_acts, ((1,), (0,)))
                parts.append(jnp.sum(mixed * rot_grads, axis=0, keepdims=True))
            score = jnp.concatenate(parts, axis=0)
            for c in range(NC):
                part = score[:, c * TOK : (c + 1) * TOK]

                @pl.when(h == 0)
                def _():
                    scores[j, c] = part

                @pl.when(h > 0)
                def _():
                    scores[j, c] = scores[j, c] + part

                @pl.when(jnp.logical_and(h == SIDE - 1, jnp.logical_not(is_self(j, c))))
                def _():
                    return_copy(j, c).start()

    home[core, 0] = scores[0, core]
    for kind in range(NC):
        for j in range(SIDE):

            def wait_home():
                pltpu.make_async_remote_copy(
                    scores.at[j, 0], home.at[kind, j], back_sem.at[j, 0], home_sem.at[kind, j],
                    device_id=holder(kind, j), device_id_type=MESH).wait_recv()

            if j == 0:
                pl.when(core != kind)(wait_home)
            else:
                wait_home()

    total = home[0, 0]
    for kind in range(NC):
        for j in range(SIDE):
            if kind + j > 0:
                total = total + home[kind, j]
    base = (z * NB + b) * TOK
    place = lax.rem(base, SEQ_LEN) + lax.broadcasted_iota(jnp.int32, (QUERIES, TOK), 1)
    out_ref[...] = jnp.where(place < lengths[lax.div(base, SEQ_LEN)], total, 0.0)

    for j in range(SIDE):
        for kind in range(NC):

            def wait_sent():
                @pl.loop(0, SIDE)
                def _(h):
                    token_copy(kind, j, h).wait_send()

                return_copy(j, kind).wait_send()

            if j == 0:
                pl.when(core != kind)(wait_sent)
            else:
                wait_sent()

    @pl.loop(0, NZ // 2)
    def _(step):
        ring(step, 1).wait_send()

    @pl.loop(0, NZ // 2 - 1)
    def _(step):
        ring(step, -1).wait_send()

    for h in range(1, SIDE):
        pltpu.make_async_remote_copy(
            weights.at[0], weights.at[h], spread_sem.at[h], held_sem.at[h],
            device_id=fellow(h), device_id_type=MESH).wait_send()


def on_device(
    train_acts, train_grads, block_table, seq_lengths,
    query_acts, query_grads, basis_acts, basis_grads, eigenvalues,
):
    bf16, f32 = jnp.bfloat16, jnp.float32
    vmem = pl.BlockSpec(memory_space=pltpu.VMEM)
    smem = pl.BlockSpec(memory_space=pltpu.SMEM)
    hbm = pl.BlockSpec(memory_space=pltpu.HBM)
    dma = pltpu.SemaphoreType.DMA
    return pl.pallas_call(
        kernel,
        out_shape=jax.ShapeDtypeStruct((QUERIES, TOK), f32),
        in_specs=[hbm] * 7 + [smem, smem],
        out_specs=vmem,
        scratch_shapes=[
            pltpu.VMEM((train_acts.shape[1] // BLOCK, TOK, BLOCK), bf16),
            pltpu.VMEM((train_grads.shape[1] // BLOCK, TOK, BLOCK), bf16),
            pltpu.VMEM((SHARD, BLOCK), f32),
            pltpu.VMEM((SIDE, NC, SIDE, TOK, 2 * BLOCK), bf16),
            pltpu.VMEM((SIDE, SIDE, NC, TOK, 2 * BLOCK), bf16),
            pltpu.VMEM((SIDE, NZ, 5 * SHARD, BLOCK), bf16),
            pltpu.VMEM((BLOCK, BLOCK), bf16),
            pltpu.VMEM((BLOCK, BLOCK), bf16),
            pltpu.VMEM((QUERIES * BLOCK, BLOCK), bf16),
            pltpu.VMEM((SIDE, NC, QUERIES, TOK), f32),
            pltpu.VMEM((NC, SIDE, QUERIES, TOK), f32),
            dma((2,)), dma((5,)), dma((SIDE, NC, SIDE)), dma((SIDE, SIDE, NC)),
            dma((NZ // 2,)), dma((NZ // 2,)), dma((NZ,)),
            dma((SIDE,)), dma((SIDE,)), dma((SIDE, NC)), dma((NC, SIDE)),
        ],
        compiler_params=pltpu.CompilerParams(
            collective_id=0, has_side_effects=True, vmem_limit_bytes=48 * 2**20),
    )(train_acts, train_grads, query_acts, query_grads, basis_acts, basis_grads, eigenvalues,
      block_table.T, seq_lengths)


def solution(mesh):
    in_specs = (
        P(("seq", "blk"), None),
        P(("seq", "blk"), None),
        P(),
        P(),
        P("blk", "seq", None),
        P("blk", "seq", None),
        P("blk", "seq", None),
        P("blk", "seq", None),
        P("blk", "seq", None),
    )
    return jax.shard_map(
        on_device, mesh=mesh, in_specs=in_specs, out_specs=P(None, ("seq", "blk")),
        check_vma=False)
```

time: 349 us -> 77 us (0.22)
  waiting for transfers between devices: 151 us -> 0 us
  blocking collectives: 115 us -> 0 us
  Pallas kernels: 0 us -> 67.9 us
  matrix products: 21.2 us -> 0 us
  local copies, waits for them, and re-layouts: 27.4 us -> 8.69 us
  between operations: 13.6 us -> 0.02 us
  starting transfers between devices: 11.5 us -> 0 us
  other arithmetic: 8.15 us -> 0 us
    unnamed x2 -> x0, waiting for transfers between devices: 151 us -> none
    all_gather x5 -> x0, blocking collectives: 115 us -> none  [the longest x1 29.4 us: on_device(): lax.all_gather(basis_acts, 'seq', axis=1, tiled=True)]
    pallas_call x0 -> x1, Pallas kernels: none -> 67.9 us  [on_device(): pl.pallas_call(kernel, out_shape=jax.ShapeDtypeStruct((QUERIES, TOK), f32...]
    dot_general x13 -> x0, matrix products: 21.2 us -> none  [the longest x8 16.6 us: block_scores(): jnp.dot(act_piece, right_mat, preferred_element_type=jnp.float32)]
    all_to_all x1 -> x0, starting transfers between devices: 11.5 us -> none  [on_device(): lax.all_to_all(slices, 'blk', split_axis=1, concat_axis=1, tiled=True)]
    reshape x2 -> x0, local copies, waits for them, and re-layouts: 6.53 us -> none  [the longest x1 6 us: on_device(): grad_blocks = train_grads.reshape(tok_dev, -1, BLOCK)]
    gather x3 -> x0, local copies, waits for them, and re-layouts: 4.63 us -> none  [the longest x1 2.72 us: on_device(): grad_sel = jnp.take(grad_blocks, block_table[:, 0], axis=1)]
    select_n x5 -> x0, other arithmetic: 4.58 us -> none  [the longest x1 1.96 us: on_device(): return jnp.where(valid[None, :], own_scores.T, jnp.zeros((), jnp.float32))]
  transfers between devices with their start and end apart: 2 -> 0, of which waited for: 1 -> 0; matrix products, arithmetic and copies ran while one was open for 1% -> 0% of each run, Pallas kernels for 0% -> 0%
where the time goes in v2:
time: 77 us; the launch traced here: 76.6 us
  Pallas kernels  67.9 us (88%)
  local copies, waits for them, and re-layouts  8.69 us (11%)
    pallas_call x1, Pallas kernels, on_device(): pl.pallas_call(kernel, out_shape=jax.ShapeDtypeStruct((QUERIES, TOK), f32...  67.9 us
    unnamed x19, local copies, waits for them, and re-layouts  8.69 us

profile of v2, /device:TPU:1, one launch (start us, length us, event | category | flops | bytes accessed | tf_op | source)
XLA Modules:
  0.0 76.6 jit_solution(14945865971681429703)
XLA Ops:
  0.0 0.0 copy-start
  0.0 2.0 %copy-done = bf16[128,14336]{1,0:T(8,128)(2,1)S(1)} copy-done((bf16[128,14336]{1,0:T(8,128)(2,1)S(1)}, bf16[128,14336]{1,0:T(8,128)(2,1)}, u32[]{:S(2)}) %copy-start) | copy-done | bytes 3670040
  2.0 0.0 copy-start.1
  2.0 1.2 %copy-done.1 = bf16[128,4096]{1,0:T(8,128)(2,1)S(1)} copy-done((bf16[128,4096]{1,0:T(8,128)(2,1)S(1)}, bf16[128,4096]{1,0:T(8,128)(2,1)}, u32[]{:S(2)}) %copy-start.1) | copy-done | bytes 1048600
  3.3 0.0 copy-start.2
  3.3 0.7 copy-done.2
  4.0 0.0 copy-start.3
  4.0 0.7 copy-done.3
  4.7 0.0 copy-start.4
  4.7 0.7 copy-done.4
  5.4 0.0 copy-start.5
  5.4 0.7 copy-done.5
  6.1 0.0 copy-start.6
  6.1 0.7 copy-done.6
  6.8 0.0 copy-start.7
  6.8 0.7 copy-done.7
  7.5 0.0 copy-start.8
  7.5 0.7 copy-done.8
  8.1 67.9 %shard_map.91 = f32[8,128]{1,0:T(8,128)S(1)} custom-call(bf16[128,4096]{1,0:T(8,128)(2,1)S(1)} %copy-done.1, bf16[128,14336]{1,0:T(8,128)(2,1)S(1)} %copy-done, bf16[1,16,256]{2,1,0:T(8,128)(2,1)S(1)} %copy-done.3, bf16[1,16,256]{2,1,0:T(8,128)(2,1)S(1)} %copy-done.4, bf16[1,16,256]{2,1,0:T(8,128)(2,1)S(1)} %copy-done.5, bf16[1,16,256]{2,1,0:T(8,128)(2,1)S(1)} %copy-done.6, ...), custom_call_target="tpu_custom_call" | custom-call | tf_op jit(solution)/shard_map/pallas_call | solution.py:291
  76.0 0.6 copy.11
Async XLA Ops:
  0.0 2.0 %copy-start = (bf16[128,14336]{1,0:T(8,128)(2,1)S(1)}, bf16[128,14336]{1,0:T(8,128)(2,1)}, u32[]{:S(2)}) copy-start(bf16[128,14336]{1,0:T(8,128)(2,1)} %grads_hbm.1) | copy-start | bytes 11010052
  2.0 1.2 %copy-start.1 = (bf16[128,4096]{1,0:T(8,128)(2,1)S(1)}, bf16[128,4096]{1,0:T(8,128)(2,1)}, u32[]{:S(2)}) copy-start(bf16[128,4096]{1,0:T(8,128)(2,1)} %acts_hbm.1) | copy-start | bytes 3145732
  3.3 0.7 copy-start.2
  4.0 0.7 copy-start.3
  4.7 0.7 copy-start.4
  5.4 0.7 copy-start.5
  6.1 0.7 copy-start.6
  6.8 0.7 copy-start.7
  7.5 0.7 copy-start.8

commit v3 on v2

--- a/solution.py
+++ b/solution.py
@@ -35,8 +35,8 @@
 def kernel(
     acts_hbm, grads_hbm, qa_hbm, qg_hbm, ba_hbm, bg_hbm, eig_hbm, table, lengths,
     out_ref,
-    acts, grads, eig, send, recv, weights, act_t, grad_t, right, scores, home,
-    load_sem, shard_sem, send_sem, recv_sem, up_sem, down_sem, ring_sem,
+    acts, grads, eig, raw, send, recv, weights, act_t, grad_t, right, scores, home,
+    load_sem, shard_sem, send_sem, recv_sem, up_sem, swap_sem, ring_sem,
     spread_sem, held_sem, back_sem, home_sem,
 ):
     z = lax.axis_index("seq")
@@ -44,23 +44,37 @@
     core = lax.rem(b, NC)
     chip = lax.div(b, NC)
     y, x = lax.div(chip, SIDE), lax.rem(chip, SIDE)
-    above, below = wrap(z + 1, NZ), wrap(z - 1, NZ)
+
+    twist = 2 * lax.rem(z, 2)
 
     def holder(kind, j):
+        if j == 2:
+            return (wrap(z + (1 if kind == 0 else NZ - 1), NZ), blk_of(y, x, kind))
         return (z, blk_of(y + j, x, 0) if kind == 0 else blk_of(y, x + j, 1))
 
     def pair(kind, j, h):
-        return blk_of(y + j, x + h, 0) if kind == 0 else blk_of(y + h, x + j, 1)
+        if kind == 0:
+            return blk_of(wrap(y + j + twist), x + h, 0)
+        return blk_of(y + h, wrap(x + j + twist), 1)
 
     def source(j, c):
-        return (z, jnp.where(core == 0, blk_of(y - j, x, c), blk_of(y, x - j, c)))
+        far = j == 2
+        plane = jnp.where(far, wrap(z + jnp.where(core == 0, NZ - 1, 1), NZ), z)
+        step = jnp.where(far, 0, SIDE - j)
+        return (plane, jnp.where(core == 0, blk_of(y + step, x, c), blk_of(y, x + step, c)))
 
     def fellow(h):
         return (z, jnp.where(core == 0, blk_of(y, x - h, 0), blk_of(y - h, x, 1)))
 
+    def beside():
+        return jnp.where(core == 0, blk_of(y + 2, x, 0), blk_of(y, x + 2, 1))
+
+    def column(to):
+        return (wrap(z + to, NZ), beside() if to % 2 else b)
+
     shards = [
         pltpu.make_async_copy(
-            hbm.at[0], weights.at[0, z, pl.ds(place * SHARD, SHARD)], shard_sem.at[place])
+            hbm.at[0], raw.at[pl.ds(place * SHARD, SHARD)], shard_sem.at[place])
         for place, hbm in enumerate((ba_hbm, bg_hbm, qa_hbm, qg_hbm))
     ] + [pltpu.make_async_copy(eig_hbm.at[0], eig, shard_sem.at[4])]
     for copy in shards:
@@ -73,46 +87,55 @@
             pltpu.make_async_copy(hbm.at[:, columns], blocks.at[block], load_sem.at[sem]).start()
 
     barrier = pltpu.get_barrier_semaphore()
-    greeted = [(z, blk_of(y, x, 1 - core)), (above, b), (below, b)]
+    greeted = [(z, blk_of(y, x, 1 - core))]
     for j in range(1, SIDE):
         for c in range(NC):
             greeted += [(z, blk_of(y + j, x, c)), (z, blk_of(y, x + j, c))]
+    for step in (2, 4, 8, NZ - 4, NZ - 2):
+        greeted.append((wrap(z + step, NZ), b))
+    for step in (1, NZ - 1):
+        greeted.append((wrap(z + step, NZ), beside()))
+        for c in range(NC):
+            greeted.append((wrap(z + step, NZ), blk_of(y, x, c)))
     for peer in greeted:
         pl.semaphore_signal(barrier, inc=1, device_id=peer, device_id_type=MESH)
 
     for copy in shards:
         copy.wait()
-    weights[0, z, 4 * SHARD : 5 * SHARD] = (eig[...] + DAMPING).astype(jnp.bfloat16)
+    raw[4 * SHARD : 5 * SHARD] = (eig[...] + DAMPING).astype(jnp.bfloat16)
     pl.semaphore_wait(barrier, len(greeted))
 
-    def ring(step, direction):
-        slot, to, sems = (
-            (wrap(z - step, NZ), above, up_sem) if direction > 0
-            else (wrap(z + step, NZ), below, down_sem))
+    def piece_copy(slot, to):
         piece = weights.at[0, slot]
         return pltpu.make_async_remote_copy(
-            piece, piece, sems.at[step], ring_sem.at[slot],
-            device_id=(to, b), device_id_type=MESH)
-
-    def arrived(slot):
-        piece = weights.at[0, slot]
-        pltpu.make_async_remote_copy(
             piece, piece, up_sem.at[0], ring_sem.at[slot],
-            device_id=(above, b), device_id_type=MESH).wait_recv()
+            device_id=column(to), device_id_type=MESH)
+
+    def arrived(step):
+        slot = wrap(z + step, NZ)
+        piece_copy(slot, 1).wait_recv()
+        return slot
+
+    def spread_copy(piece, h):
+        return pltpu.make_async_remote_copy(
+            weights.at[0, piece], weights.at[h, piece], spread_sem.at[h], held_sem.at[h],
+            device_id=fellow(h), device_id_type=MESH)
 
     def spread(slot):
-        for h in range(1, SIDE):
-            pltpu.make_async_remote_copy(
-                weights.at[0, slot], weights.at[h, slot], spread_sem.at[h], held_sem.at[h],
-                device_id=fellow(h), device_id_type=MESH).start()
+        for h in (1, 3):
+            spread_copy(slot, h).start()
+
+    swap = pltpu.make_async_remote_copy(
+        raw, weights.at[0, z], swap_sem.at[0], ring_sem.at[z],
+        device_id=(z, beside()), device_id_type=MESH)
 
     def token_copy(kind, j, h):
         return pltpu.make_async_remote_copy(
             send.at[h, kind, j], recv.at[h, j, core], send_sem.at[h, kind, j],
             recv_sem.at[h, j, core], device_id=holder(kind, j), device_id_type=MESH)
 
-    def dispatch(h):
-        for j in (0, 2, 1, 3):
+    def dispatch(h, offsets):
+        for j in offsets:
             for kind in range(NC):
                 owner = pair(kind, j, h)
                 act_sel, grad_sel = acts[table[1, owner]], grads[table[0, owner]]
@@ -132,31 +155,39 @@
                 else:
                     to_peer()
 
-    ring(0, 1).start()
-    ring(0, -1).start()
-    spread(z)
+    def hand_on(slot, steps):
+        for to in steps:
+            piece_copy(slot, to).start()
+        spread(slot)
+
+    @pl.when(twist > 0)
+    def _():
+        swap.start()
+        swap.wait()
+
+    @pl.when(twist == 0)
+    def _():
+        weights[0, z] = raw[...]
+
+    hand_on(z, (4, NZ - 4, 8, 1, NZ - 1, 2, NZ - 2))
     for blocks, sem in ((acts, 0), (grads, 1)):
         pltpu.make_async_copy(blocks, blocks, load_sem.at[sem]).wait()
-
-    @pl.loop(1, NZ // 2)
-    def _(step):
-        @pl.when(step <= SIDE)
-        def _():
-            dispatch(step - 1)
-
-        arrived(wrap(z - step, NZ))
-        ring(step, 1).start()
-        arrived(wrap(z + step, NZ))
-
-        @pl.when(step < NZ // 2 - 1)
-        def _():
-            ring(step, -1).start()
-
-        spread(wrap(z - step, NZ))
-        spread(wrap(z + step, NZ))
-
-    arrived(wrap(z + NZ // 2, NZ))
-    spread(wrap(z + NZ // 2, NZ))
+    dispatch(0, (0, 1, 3))
+    dispatch(1, (0, 1, 3))
+    for step in (4, NZ - 4):
+        hand_on(arrived(step), (1, NZ - 1))
+    hand_on(arrived(8), (1, NZ - 1, 2, NZ - 2))
+    dispatch(0, (2,))
+    dispatch(1, (2,))
+    dispatch(3, (0, 1, 3))
+    for step in (1, NZ - 1, 2, NZ - 2):
+        spread(arrived(step))
+    dispatch(3, (2,))
+    dispatch(2, (0, 1, 3, 2))
+    for step in (5, 13, 3, 11, 9, 7, 10, 6):
+        spread(arrived(step))
+    every = pl.ds(0, NZ)
+    spread_copy(every, 2).start()
 
     def prepare(h):
         def gathered(place):
@@ -183,12 +214,12 @@
         return jnp.logical_and(j == 0, c == core)
 
     @pl.loop(0, SIDE)
-    def _(h):
+    def _(turn):
+        h = lax.rem(turn * (turn + 1) // 2, SIDE)
+
         @pl.when(h > 0)
         def _():
-            pltpu.make_async_remote_copy(
-                weights.at[0], weights.at[h], spread_sem.at[h], held_sem.at[h],
-                device_id=fellow(h), device_id_type=MESH).wait_recv()
+            spread_copy(every, h).wait_recv()
 
         prepare(h)
 
@@ -215,15 +246,15 @@
             for c in range(NC):
                 part = score[:, c * TOK : (c + 1) * TOK]
 
-                @pl.when(h == 0)
+                @pl.when(turn == 0)
                 def _():
                     scores[j, c] = part
 
-                @pl.when(h > 0)
+                @pl.when(turn > 0)
                 def _():
                     scores[j, c] = scores[j, c] + part
 
-                @pl.when(jnp.logical_and(h == SIDE - 1, jnp.logical_not(is_self(j, c))))
+                @pl.when(jnp.logical_and(turn == SIDE - 1, jnp.logical_not(is_self(j, c))))
                 def _():
                     return_copy(j, c).start()
 
@@ -265,18 +296,12 @@
             else:
                 wait_sent()
 
-    @pl.loop(0, NZ // 2)
-    def _(step):
-        ring(step, 1).wait_send()
-
-    @pl.loop(0, NZ // 2 - 1)
-    def _(step):
-        ring(step, -1).wait_send()
-
+    gone = weights.at[0, pl.ds(0, NZ - 1)]
+    pltpu.make_async_remote_copy(
+        gone, gone, up_sem.at[0], ring_sem.at[0], device_id=(wrap(z + 1, NZ), b),
+        device_id_type=MESH).wait_send()
     for h in range(1, SIDE):
-        pltpu.make_async_remote_copy(
-            weights.at[0], weights.at[h], spread_sem.at[h], held_sem.at[h],
-            device_id=fellow(h), device_id_type=MESH).wait_send()
+        spread_copy(every, h).wait_send()
 
 
 def on_device(
@@ -297,6 +322,7 @@
             pltpu.VMEM((train_acts.shape[1] // BLOCK, TOK, BLOCK), bf16),
             pltpu.VMEM((train_grads.shape[1] // BLOCK, TOK, BLOCK), bf16),
             pltpu.VMEM((SHARD, BLOCK), f32),
+            pltpu.VMEM((5 * SHARD, BLOCK), bf16),
             pltpu.VMEM((SIDE, NC, SIDE, TOK, 2 * BLOCK), bf16),
             pltpu.VMEM((SIDE, SIDE, NC, TOK, 2 * BLOCK), bf16),
             pltpu.VMEM((SIDE, NZ, 5 * SHARD, BLOCK), bf16),
@@ -306,11 +332,11 @@
             pltpu.VMEM((SIDE, NC, QUERIES, TOK), f32),
             pltpu.VMEM((NC, SIDE, QUERIES, TOK), f32),
             dma((2,)), dma((5,)), dma((SIDE, NC, SIDE)), dma((SIDE, SIDE, NC)),
-            dma((NZ // 2,)), dma((NZ // 2,)), dma((NZ,)),
+            dma((1,)), dma((1,)), dma((NZ,)),
             dma((SIDE,)), dma((SIDE,)), dma((SIDE, NC)), dma((NC, SIDE)),
         ],
         compiler_params=pltpu.CompilerParams(
-            collective_id=0, has_side_effects=True, vmem_limit_bytes=48 * 2**20),
+            collective_id=0, has_side_effects=True, vmem_limit_bytes=63 * 2**20),
     )(train_acts, train_grads, query_acts, query_grads, basis_acts, basis_grads, eigenvalues,
       block_table.T, seq_lengths)
 

time: 77 us -> 65.9 us (0.86)
  local copies, waits for them, and re-layouts: 8.69 us -> 1.28 us
  Pallas kernels: 67.9 us -> 64.5 us
    unnamed x19 -> x1, local copies, waits for them, and re-layouts: 8.69 us -> 1.28 us
    pallas_call x1, Pallas kernels: 67.9 us -> 64.5 us  [on_device(): pl.pallas_call(kernel, out_shape=jax.ShapeDtypeStruct((QUERIES, TOK), f32...]
where the time goes in v3:
time: 65.9 us; the launch traced here: 65.8 us
  Pallas kernels  64.5 us (98%)
  local copies, waits for them, and re-layouts  1.28 us (2%)
    pallas_call x1, Pallas kernels, on_device(): pl.pallas_call(kernel, out_shape=jax.ShapeDtypeStruct((QUERIES, TOK), f32...  64.5 us

profile of v3, /device:TPU:1, one launch (start us, length us, event | category | flops | bytes accessed | tf_op | source)
XLA Modules:
  0.0 65.8 jit_solution(9835394705313714043)
XLA Ops:
  0.0 64.5 %shard_map.91 = f32[8,128]{1,0:T(8,128)} custom-call(bf16[128,4096]{1,0:T(8,128)(2,1)} %acts_hbm.1, bf16[128,14336]{1,0:T(8,128)(2,1)} %grads_hbm.1, bf16[1,16,256]{2,1,0:T(8,128)(2,1)} %qa_hbm.1, bf16[1,16,256]{2,1,0:T(8,128)(2,1)} %qg_hbm.1, bf16[1,16,256]{2,1,0:T(8,128)(2,1)} %ba_hbm.1, bf16[1,16,256]{2,1,0:T(8,128)(2,1)} %bg_hbm.1, ...), custom_call_target="tpu_custom_call" | custom-call | tf_op jit(solution)/shard_map/pallas_call | solution.py:316
  64.5 1.3 %copy.11 = f32[8,128]{1,0:T(8,128)} copy(f32[8,128]{1,0:T(8,128)} %shard_map.91) | data formatting | bytes 8192

commit v4 on v3

--- a/solution.py
+++ b/solution.py
@@ -79,13 +79,6 @@
     ] + [pltpu.make_async_copy(eig_hbm.at[0], eig, shard_sem.at[4])]
     for copy in shards:
         copy.start()
-    for hbm, blocks, sem in ((acts_hbm, acts, 0), (grads_hbm, grads, 1)):
-
-        @pl.loop(0, blocks.shape[0])
-        def _(block):
-            columns = pl.ds(pl.multiple_of(block * BLOCK, BLOCK), BLOCK)
-            pltpu.make_async_copy(hbm.at[:, columns], blocks.at[block], load_sem.at[sem]).start()
-
     barrier = pltpu.get_barrier_semaphore()
     greeted = [(z, blk_of(y, x, 1 - core))]
     for j in range(1, SIDE):
@@ -99,6 +92,13 @@
             greeted.append((wrap(z + step, NZ), blk_of(y, x, c)))
     for peer in greeted:
         pl.semaphore_signal(barrier, inc=1, device_id=peer, device_id_type=MESH)
+
+    for hbm, blocks, sem in ((acts_hbm, acts, 0), (grads_hbm, grads, 1)):
+
+        @pl.loop(0, blocks.shape[0])
+        def _(block):
+            columns = pl.ds(pl.multiple_of(block * BLOCK, BLOCK), BLOCK)
+            pltpu.make_async_copy(hbm.at[:, columns], blocks.at[block], load_sem.at[sem]).start()
 
     for copy in shards:
         copy.wait()
@@ -224,7 +224,8 @@
         prepare(h)
 
         @pl.loop(0, SIDE)
-        def _(j):
+        def _(place):
+            j = lax.rem(2 + 3 * place, SIDE)
             for c in range(NC):
 
                 @pl.when(jnp.logical_not(is_self(j, c)))

time: 65.9 us -> 63.9 us (0.970)
  Pallas kernels: 64.5 us -> 62.4 us
    pallas_call x1, Pallas kernels: 64.5 us -> 62.4 us  [on_device(): pl.pallas_call(kernel, out_shape=jax.ShapeDtypeStruct((QUERIES, TOK), f32...]
where the time goes in v4:
time: 63.9 us; the launch traced here: 63.7 us
  Pallas kernels  62.4 us (98%)
  local copies, waits for them, and re-layouts  1.28 us (2%)
    pallas_call x1, Pallas kernels, on_device(): pl.pallas_call(kernel, out_shape=jax.ShapeDtypeStruct((QUERIES, TOK), f32...  62.4 us

profile of v4, /device:TPU:1, one launch (start us, length us, event | category | flops | bytes accessed | tf_op | source)
XLA Modules:
  0.0 63.7 jit_solution(9646629366155416266)
XLA Ops:
  0.0 62.4 %shard_map.91 = f32[8,128]{1,0:T(8,128)} custom-call(bf16[128,4096]{1,0:T(8,128)(2,1)} %acts_hbm.1, bf16[128,14336]{1,0:T(8,128)(2,1)} %grads_hbm.1, bf16[1,16,256]{2,1,0:T(8,128)(2,1)} %qa_hbm.1, bf16[1,16,256]{2,1,0:T(8,128)(2,1)} %qg_hbm.1, bf16[1,16,256]{2,1,0:T(8,128)(2,1)} %ba_hbm.1, bf16[1,16,256]{2,1,0:T(8,128)(2,1)} %bg_hbm.1, ...), custom_call_target="tpu_custom_call" | custom-call | tf_op jit(solution)/shard_map/pallas_call | solution.py:317
  62.4 1.3 %copy.11 = f32[8,128]{1,0:T(8,128)} copy(f32[8,128]{1,0:T(8,128)} %shard_map.91) | data formatting | bytes 8192

commit v5 on v4

--- a/solution.py
+++ b/solution.py
@@ -174,12 +174,12 @@
         pltpu.make_async_copy(blocks, blocks, load_sem.at[sem]).wait()
     dispatch(0, (0, 1, 3))
     dispatch(1, (0, 1, 3))
+    dispatch(3, (0, 1, 3))
     for step in (4, NZ - 4):
         hand_on(arrived(step), (1, NZ - 1))
     hand_on(arrived(8), (1, NZ - 1, 2, NZ - 2))
     dispatch(0, (2,))
     dispatch(1, (2,))
-    dispatch(3, (0, 1, 3))
     for step in (1, NZ - 1, 2, NZ - 2):
         spread(arrived(step))
     dispatch(3, (2,))

time: 63.9 us -> 63.8 us (level)
  the two profiles are of different devices: /device:TPU:1 before, /device:TPU:33 now
where the time goes in v5:
time: 63.8 us; the launch traced here: 63.6 us
  Pallas kernels  62.3 us (98%)
  local copies, waits for them, and re-layouts  1.28 us (2%)
    pallas_call x1, Pallas kernels, on_device(): pl.pallas_call(kernel, out_shape=jax.ShapeDtypeStruct((QUERIES, TOK), f32...  62.3 us

profile of v5, /device:TPU:33, one launch (start us, length us, event | category | flops | bytes accessed | tf_op | source)
XLA Modules:
  0.0 63.6 jit_solution(16498897013105633901)
XLA Ops:
  0.0 62.3 %shard_map.91 = f32[8,128]{1,0:T(8,128)} custom-call(bf16[128,4096]{1,0:T(8,128)(2,1)} %acts_hbm.1, bf16[128,14336]{1,0:T(8,128)(2,1)} %grads_hbm.1, bf16[1,16,256]{2,1,0:T(8,128)(2,1)} %qa_hbm.1, bf16[1,16,256]{2,1,0:T(8,128)(2,1)} %qg_hbm.1, bf16[1,16,256]{2,1,0:T(8,128)(2,1)} %ba_hbm.1, bf16[1,16,256]{2,1,0:T(8,128)(2,1)} %bg_hbm.1, ...), custom_call_target="tpu_custom_call" | custom-call | tf_op jit(solution)/shard_map/pallas_call | solution.py:317
  62.3 1.3 %copy.11 = f32[8,128]{1,0:T(8,128)} copy(f32[8,128]{1,0:T(8,128)} %shard_map.91) | data formatting | bytes 8192
